TPU v7x, 32 devices: a whole 2x2x4 slice. The times are simulated.
32 devices in a mesh: dp: 8 (over y, x, core), tensor: 4 (over z).
Axes of the slice: x: 2, y: 2, z: 4, core: 2. Of those that a mesh axis runs over, the one named last changes fastest.
Arguments:
- grad_inproj: bfloat16 [8, 768, 2304], P('dp', None, 'tensor'), may hold values from -32 to 32
- error_inproj: float32 [8, 768, 2304], P('dp', None, 'tensor'), may hold values from -3 to 3
- basis_inproj: float32 [2304, 32], P('tensor'), may hold values from -6 to 6
- weight_inproj: float32 [768, 2304], P('dp', 'tensor'), may hold values from -0.3 to 0.3
- moment_inproj: float32 [768, 2304], P('dp', 'tensor'), may hold values from -0.3 to 0.3
- grad_outproj: bfloat16 [8, 768, 768], P('dp', 'tensor'), may hold values from -32 to 32
- error_outproj: float32 [8, 768, 768], P('dp', 'tensor'), may hold values from -3 to 3
- basis_outproj: float32 [768, 32], replicated, may hold values from -6 to 6
- weight_outproj: float32 [768, 768], P(('tensor', 'dp')), may hold values from -0.3 to 0.3
- moment_outproj: float32 [768, 768], P(('tensor', 'dp')), may hold values from -0.3 to 0.3
- grad_expand: bfloat16 [8, 768, 3072], P('dp', None, 'tensor'), may hold values from -32 to 32
- error_expand: float32 [8, 768, 3072], P('dp', None, 'tensor'), may hold values from -3 to 3
- basis_expand: float32 [3072, 32], P('tensor'), may hold values from -6 to 6
- weight_expand: float32 [768, 3072], P('dp', 'tensor'), may hold values from -0.3 to 0.3
- moment_expand: float32 [768, 3072], P('dp', 'tensor'), may hold values from -0.3 to 0.3
- grad_contract: bfloat16 [8, 3072, 768], P('dp', 'tensor'), may hold values from -32 to 32
- error_contract: float32 [8, 3072, 768], P('dp', 'tensor'), may hold values from -3 to 3
- basis_contract: float32 [768, 32], replicated, may hold values from -6 to 6
- weight_contract: float32 [3072, 768], P(('tensor', 'dp')), may hold values from -0.3 to 0.3
- moment_contract: float32 [3072, 768], P(('tensor', 'dp')), may hold values from -0.3 to 0.3
Outputs:
- residue_inproj: float32 [8, 768, 2304], P('dp', None, 'tensor')
- factor_inproj: float32 [2304, 32], P('tensor')
- master_inproj: float32 [768, 2304], P('dp', 'tensor')
- velocity_inproj: float32 [768, 2304], P('dp', 'tensor')
- serving_inproj: bfloat16 [768, 2304], P(None, 'tensor')
- residue_outproj: float32 [8, 768, 768], P('dp', 'tensor')
- factor_outproj: float32 [768, 32], replicated
- master_outproj: float32 [768, 768], P(('tensor', 'dp'))
- velocity_outproj: float32 [768, 768], P(('tensor', 'dp'))
- serving_outproj: bfloat16 [768, 768], P('tensor')
- residue_expand: float32 [8, 768, 3072], P('dp', None, 'tensor')
- factor_expand: float32 [3072, 32], P('tensor')
- master_expand: float32 [768, 3072], P('dp', 'tensor')
- velocity_expand: float32 [768, 3072], P('dp', 'tensor')
- serving_expand: bfloat16 [768, 3072], P(None, 'tensor')
- residue_contract: float32 [8, 3072, 768], P('dp', 'tensor')
- factor_contract: float32 [768, 32], replicated
- master_contract: float32 [3072, 768], P(('tensor', 'dp'))
- velocity_contract: float32 [3072, 768], P(('tensor', 'dp'))
- serving_contract: bfloat16 [3072, 768], P('tensor')
All inputs are finite; a program needn't handle non-finite values.
Results may differ from a plain program's by a relative error of at most 0.012.
Values may be sent and summed in bfloat16 or wider, within the bound.
A program may use at most 128 MiB of HBM per device.

v0:
```python
import jax
import jax.numpy as jnp
from jax import lax
from jax.sharding import PartitionSpec as P

NS_STEPS = 5
momentum_beta = 0.9
step_size = 0.05


def matmul_high(left, right):
    return jnp.dot(left, right, precision=lax.Precision.HIGHEST, preferred_element_type=jnp.float32)


def inverse_root(gram):
    identity = jnp.eye(gram.shape[0], dtype=jnp.float32)
    norm_total = jnp.sqrt(jnp.sum(gram * gram)) + 1e-06
    iter_y = gram / norm_total
    iter_z = identity
    for repeat in range(NS_STEPS):
        middle = 1.5 * identity - 0.5 * matmul_high(iter_z, iter_y)
        iter_y = matmul_high(iter_y, middle)
        iter_z = matmul_high(middle, iter_z)
    return iter_z / jnp.sqrt(norm_total)


def own_rows(approx, weight):
    height = weight.shape[0]
    start = lax.axis_index("dp") * height
    return lax.dynamic_slice_in_dim(approx, start, height, 0)


def pair_update(col_group, row_group):
    grad_col, error_col, basis_col, weight_col, moment_col = col_group
    grad_row, error_row, basis_row, weight_row, moment_row = row_group
    replicas = lax.axis_size("dp")
    merged_col = grad_col[0].astype(jnp.float32) + error_col[0]
    merged_row = grad_row[0].astype(jnp.float32) + error_row[0]
    part_col = matmul_high(merged_col, basis_col)
    part_row = matmul_high(merged_row, basis_row)
    left_col = lax.psum(part_col, ("dp", "tensor")) / replicas
    left_row = lax.psum(part_row, "dp") / replicas
    gram_row = lax.psum(matmul_high(left_row.T, left_row), "tensor")
    gram_col = matmul_high(left_col.T, left_col)
    normed_col = matmul_high(left_col, inverse_root(gram_col))
    normed_row = matmul_high(left_row, inverse_root(gram_row))
    factor_col = (
        lax.psum(matmul_high(merged_col.T, normed_col).astype(jnp.bfloat16), "dp").astype(
            jnp.float32
        )
        / replicas
    )
    factor_row = lax.psum(matmul_high(merged_row.T, normed_row), ("dp", "tensor")) / replicas
    approx_col = matmul_high(normed_col, factor_col.T)
    approx_row = matmul_high(normed_row, factor_row.T)
    residue_col = (merged_col - approx_col)[None]
    residue_row = (merged_row - approx_row)[None]
    velocity_col = momentum_beta * moment_col + own_rows(approx_col, weight_col)
    velocity_row = momentum_beta * moment_row + own_rows(approx_row, weight_row)
    master_col = weight_col - step_size * velocity_col
    master_row = weight_row - step_size * velocity_row
    serving_col, serving_row = (
        lax.all_gather(master_col.astype(jnp.bfloat16), "dp", axis=0, tiled=True),
        lax.all_gather(master_row.astype(jnp.bfloat16), "dp", axis=0, tiled=True),
    )
    return (
        (residue_col, factor_col, master_col, velocity_col, serving_col),
        (residue_row, factor_row, master_row, velocity_row, serving_row),
    )


def body(
    grad_inproj,
    error_inproj,
    basis_inproj,
    weight_inproj,
    moment_inproj,
    grad_outproj,
    error_outproj,
    basis_outproj,
    weight_outproj,
    moment_outproj,
    grad_expand,
    error_expand,
    basis_expand,
    weight_expand,
    moment_expand,
    grad_contract,
    error_contract,
    basis_contract,
    weight_contract,
    moment_contract,
):
    first, second = pair_update(
        (grad_inproj, error_inproj, basis_inproj, weight_inproj, moment_inproj),
        (grad_outproj, error_outproj, basis_outproj, weight_outproj, moment_outproj),
    )
    third, fourth = pair_update(
        (grad_expand, error_expand, basis_expand, weight_expand, moment_expand),
        (grad_contract, error_contract, basis_contract, weight_contract, moment_contract),
    )
    return (
        first[0],
        first[1],
        first[2],
        first[3],
        first[4],
        second[0],
        second[1],
        second[2],
        second[3],
        second[4],
        third[0],
        third[1],
        third[2],
        third[3],
        third[4],
        fourth[0],
        fourth[1],
        fourth[2],
        fourth[3],
        fourth[4],
    )


def solution(mesh):
    in_specs = (
        P("dp", None, "tensor"),
        P("dp", None, "tensor"),
        P("tensor", None),
        P("dp", "tensor"),
        P("dp", "tensor"),
        P("dp", "tensor", None),
        P("dp", "tensor", None),
        P(),
        P(("tensor", "dp"), None),
        P(("tensor", "dp"), None),
        P("dp", None, "tensor"),
        P("dp", None, "tensor"),
        P("tensor", None),
        P("dp", "tensor"),
        P("dp", "tensor"),
        P("dp", "tensor", None),
        P("dp", "tensor", None),
        P(),
        P(("tensor", "dp"), None),
        P(("tensor", "dp"), None),
    )
    out_specs = (
        P("dp", None, "tensor"),
        P("tensor", None),
        P("dp", "tensor"),
        P("dp", "tensor"),
        P(None, "tensor"),
        P("dp", "tensor", None),
        P(),
        P(("tensor", "dp"), None),
        P(("tensor", "dp"), None),
        P("tensor", None),
        P("dp", None, "tensor"),
        P("tensor", None),
        P("dp", "tensor"),
        P("dp", "tensor"),
        P(None, "tensor"),
        P("dp", "tensor", None),
        P(),
        P(("tensor", "dp"), None),
        P(("tensor", "dp"), None),
        P("tensor", None),
    )
    return jax.shard_map(body, mesh=mesh, in_specs=in_specs, out_specs=out_specs, check_vma=False)
```

profile of v0, /device:TPU:0, one launch (start us, length us, event | category | flops | bytes accessed | tf_op | source)
XLA Modules:
  0.0 365.6 jit_solution(10655994586328658243)
XLA Ops:
  8.1 5.1 %fusion.2 = f32[768,32]{0,1:T(8,128)} fusion(f32[768,32]{0,1:T(8,128)S(1)} %copy-done, f32[1,768,768]{2,1,0:T(8,128)} %param.36, bf16[1,768,768]{2,1,0:T(8,128)(2,1)} %param.35), kind=kOutput, calls=%fused_computation.3 | convolution fusion | flops 227672064 | bytes 3735552 | tf_op jit(solution)/shard_map/dot_general | solution.py:12
  14.9 25.5 %psum.72 = f32[192,32]{0,1:T(8,128)S(1)} all-reduce(f32[192,32]{0,1:T(8,128)S(1)} %fusion.43), channel_id=1, replica_groups=mesh['dp'=8,'tensor'=4] {'dp'}, use_global_device_ids=true, to_apply=%region_3.0 | all-reduce | flops 6144 | bytes 49152 | tf_op jit(solution)/shard_map/psum | solution.py:42
  40.4 1.9 fusion.12
  42.3 5.1 %fusion.7 = f32[768,32]{0,1:T(8,128)} fusion(f32[768,32]{0,1:T(8,128)} %param.32, f32[1,768,768]{2,1,0:T(8,128)} %param.31, bf16[1,768,768]{2,1,0:T(8,128)(2,1)} %param.30), kind=kOutput, calls=%fused_computation.9 | convolution fusion | flops 227672064 | bytes 3735552 | tf_op jit(solution)/shard_map/dot_general | solution.py:12
  47.6 20.0 %all-reduce.7.cloned.1.call-done = f32[768,32]{0,1:T(8,128)} async-done(((f32[768,32]{0,1:T(8,128)}), f32[768,32]{0,1:T(8,128)}) %all-reduce.7.cloned.1.call-update) | async-done | bytes 98320 | tf_op jit(solution)/shard_map/psum | solution.py:42
  68.8 19.0 %all-reduce.1 = (f32[32,32]{1,0:T(8,128)S(1)}, f32[32,32]{1,0:T(8,128)S(1)}) all-reduce(f32[32,32]{1,0:T(8,128)S(1)} %fusion.66, f32[32,32]{1,0:T(8,128)S(1)} %fusion.48), channel_id=1, replica_groups=mesh['dp'=8,'tensor'=4] {'tensor'}, use_global_device_ids=true, to_apply=%region_4.0 | all-reduce | flops 2048 | bytes 16384 | tf_op jit(solution)/shard_map/psum | solution.py:43
  95.0 3.5 fusion
  101.1 126.5 %all-reduce.9.cloned.1.call-done = (f32[768,32]{0,1:T(8,128)}, f32[768,32]{0,1:T(8,128)}, f32[768,32]{0,1:T(8,128)}, f32[768,32]{0,1:T(8,128)}) async-done(((f32[768,32]{0,1:T(8,128)}, f32[768,32]{0,1:T(8,128)}, f32[768,32]{0,1:T(8,128)}, f32[768,32]{0,1:T(8,128)}), (f32[768,32]{0,1:T(8,128)}, f32[768,32]{0,1:T(8,128)}, f32[768,32]{0,1:T(8,128)}, f32[768,32]{0,1:T(8,128)})) %all-reduce.9.cloned.1.call-update) | async-done | bytes 393232 | tf_op jit(solution)/shard_map/psum | solution.py:41
  231.9 1.8 multiply_reduce_fusion.3
  237.9 4.3 %fusion.15 = bf16[768,32]{0,1:T(8,128)(2,1)} fusion(f32[768,32]{0,1:T(8,128)S(1)} %fusion.50, f32[1,768,768]{2,1,0:T(8,128)} %param.31, bf16[1,768,768]{2,1,0:T(8,128)(2,1)} %param.30), kind=kOutput, calls=%fused_computation.21 | convolution fusion | flops 227696640 | bytes 3686400 | tf_op jit(solution)/shard_map/dot_general | solution.py:12
  243.7 2.3 fusion.18
  247.5 3.5 fusion.117
  251.1 2.1 fusion.86
  253.2 1.8 copy.44
  255.0 1.8 copy.45
  261.6 3.8 %fusion.4 = f32[1,768,768]{2,1,0:T(8,128)} fusion(f32[768,768]{1,0:T(8,128)} %fusion.117, f32[1,768,768]{2,1,0:T(8,128)S(1)} %copy-done.1, bf16[1,768,768]{2,1,0:T(8,128)(2,1)} %param.35), kind=kLoop, calls=%fused_computation.5 | loop fusion | flops 1769472 | bytes 8257536 | tf_op jit(solution)/shard_map/broadcast_in_dim | solution.py:57
  265.4 35.7 %all-reduce.11.cloned.1.call-done = (bf16[576,32]{0,1:T(8,128)(2,1)}, bf16[768,32]{0,1:T(8,128)(2,1)}) async-done(((bf16[576,32]{0,1:T(8,128)(2,1)}, bf16[768,32]{0,1:T(8,128)(2,1)}), (bf16[576,32]{0,1:T(8,128)(2,1)}, bf16[768,32]{0,1:T(8,128)(2,1)})) %all-reduce.11.cloned.1.call-update) | async-done | bytes 86032 | tf_op jit(solution)/shard_map/psum | solution.py:48
  302.7 2.1 fusion.110
  305.9 11.7 %all_gather.13 = bf16[192,768]{1,0:T(8,128)(2,1)} all-gather(bf16[24,768]{1,0:T(8,128)(2,1)} %get-tuple-element.74), channel_id=1, replica_groups=mesh['dp'=8,'tensor'=4] {'dp'}, dimensions={0}, use_global_device_ids=true | all-gather | bytes 331776 | tf_op jit(solution)/shard_map/all_gather | solution.py:64
  317.6 2.2 fusion.45
  324.4 10.8 %all_gather.12 = bf16[768,576]{1,0:T(8,128)(2,1)S(1)} all-gather(bf16[96,576]{1,0:T(8,128)(2,1)S(1)} %copy.46), channel_id=1, replica_groups=mesh['dp'=8,'tensor'=4] {'dp'}, dimensions={0}, use_global_device_ids=true | all-gather | bytes 995328 | tf_op jit(solution)/shard_map/all_gather | solution.py:63
  338.2 3.7 %fusion.14 = f32[1,768,576]{1,2,0:T(8,128)} fusion(f32[768,576]{0,1:T(8,128)} %copy-done.8, f32[1,768,576]{1,2,0:T(8,128)} %param.21, bf16[1,768,576]{1,2,0:T(8,128)(2,1)S(1)} %copy-done.9), kind=kLoop, calls=%fused_computation.19 | loop fusion | flops 1327104 | bytes 6193152 | tf_op jit(solution)/shard_map/broadcast_in_dim | solution.py:56
  344.4 10.6 %all-gather.3.cloned.1.call-done = bf16[768,768]{1,0:T(8,128)(2,1)} async-done(((bf16[96,768]{1,0:T(8,128)(2,1)}), bf16[768,768]{1,0:T(8,128)(2,1)}) %all-gather.3.cloned.1.call-update) | async-done | bytes 1179664 | tf_op jit(solution)/shard_map/all_gather | solution.py:63
  355.7 2.4 copy.61
  (155 shorter events, 41.1 us)
Async XLA Ops:
  7.2 6.1 %copy-start.10 = (f32[1,192,768]{2,1,0:T(8,128)S(1)}, f32[1,192,768]{2,1,0:T(8,128)}, u32[]{:S(2)}) copy-start(f32[1,192,768]{2,1,0:T(8,128)} %param.26) | copy-start | bytes 1769476
  7.2 6.1 %copy-start.29 = (f32[768,32]{0,1:T(8,128)S(1)}, f32[768,32]{0,1:T(8,128)}, u32[]{:S(2)}) copy-start(f32[768,32]{0,1:T(8,128)} %param.27) | copy-start | bytes 294916
  7.2 33.2 %copy-start.9 = (bf16[1,768,576]{1,2,0:T(8,128)(2,1)S(1)}, bf16[1,768,576]{1,2,0:T(8,128)(2,1)}, u32[]{:S(2)}) copy-start(bf16[1,768,576]{1,2,0:T(8,128)(2,1)} %param.20) | copy-start | bytes 2654212
  7.2 33.2 %copy-start.3 = (f32[1,768,576]{1,2,0:T(8,128)S(1)}, f32[1,768,576]{1,2,0:T(8,128)}, u32[]{:S(2)}) copy-start(f32[1,768,576]{1,2,0:T(8,128)} %param.21) | copy-start | bytes 5308420
  7.3 33.2 %copy-start.30 = (f32[576,32]{0,1:T(8,128)S(1)}, f32[576,32]{0,1:T(8,128)}, u32[]{:S(2)}) copy-start(f32[576,32]{0,1:T(8,128)} %param.22) | copy-start | bytes 221188
  7.3 60.3 %all-reduce.7.cloned.1.call-start = ((), (), s32[]{:S(2)}) async-start(), calls=%async_computation.1 | async-start | bytes 196608 | tf_op jit(solution)/shard_map/psum | solution.py:42
  13.2 214.3 %all-reduce.9.cloned.1.call-start = ((), (), s32[]{:S(2)}) async-start(), calls=%async_computation.3 | async-start | bytes 786432 | tf_op jit(solution)/shard_map/psum | solution.py:41
  42.3 52.7 %copy-start.1 = (f32[1,768,768]{2,1,0:T(8,128)S(1)}, f32[1,768,768]{2,1,0:T(8,128)}, u32[]{:S(2)}) copy-start(f32[1,768,768]{2,1,0:T(8,128)} %param.36) | copy-start | bytes 7077892
  93.5 6.2 %copy-start.11 = (f32[1,192,768]{2,1,0:T(8,128)S(1)}, f32[1,192,768]{2,1,0:T(8,128)}, u32[]{:S(2)}) copy-start(f32[1,192,768]{2,1,0:T(8,128)} %param.26) | copy-start | bytes 1769476
  93.5 6.2 %copy-start.13 = (bf16[1,192,768]{2,1,0:T(8,128)(2,1)S(1)}, bf16[1,192,768]{2,1,0:T(8,128)(2,1)}, u32[]{:S(2)}) copy-start(bf16[1,192,768]{2,1,0:T(8,128)(2,1)} %param.25) | copy-start | bytes 884740
  100.9 200.3 %all-reduce.11.cloned.1.call-start = ((), (), s32[]{:S(2)}) async-start(), calls=%async_computation.4 | async-start | bytes 180224 | tf_op jit(solution)/shard_map/psum | solution.py:48
  236.3 7.4 %copy-start.4 = (f32[1,768,576]{1,2,0:T(8,128)S(1)}, f32[1,768,576]{1,2,0:T(8,128)}, u32[]{:S(2)}) copy-start(f32[1,768,576]{1,2,0:T(8,128)} %param.21) | copy-start | bytes 5308420
  237.9 4.4 %copy-start.20 = (f32[768,32]{0,1:T(8,128)}, f32[768,32]{0,1:T(8,128)S(1)}, u32[]{:S(2)}) copy-start(f32[768,32]{0,1:T(8,128)S(1)} %fusion.50) | copy-start | bytes 294916
  251.0 93.3 %all-gather.5.cloned.1.call-start = ((), (), s32[]{:S(2)}) async-start(), calls=%async_computation.2 | async-start | bytes 1327104 | tf_op jit(solution)/shard_map/all_gather | solution.py:64
  253.2 101.9 %all-gather.3.cloned.1.call-start = ((), (), s32[]{:S(2)}) async-start(), calls=%async_computation | async-start | bytes 1327104 | tf_op jit(solution)/shard_map/all_gather | solution.py:63
  261.6 41.0 %copy-start.21 = (f32[768,32]{0,1:T(8,128)S(1)}, f32[768,32]{0,1:T(8,128)}, u32[]{:S(2)}) copy-start(f32[768,32]{0,1:T(8,128)} %copy-done.20) | copy-start | bytes 294916
  304.8 18.1 %copy-start.5 = (f32[768,768]{1,0:T(8,128)}, f32[768,768]{1,0:T(8,128)S(1)}, u32[]{:S(2)}) copy-start(f32[768,768]{1,0:T(8,128)S(1)} %fusion.110) | copy-start | bytes 7077892
  305.9 17.0 %copy-start.16 = (f32[96,576]{0,1:T(8,128)S(1)}, f32[96,576]{0,1:T(8,128)}, u32[]{:S(2)}) copy-start(f32[96,576]{0,1:T(8,128)} %copy.44) | copy-start | bytes 663556
  305.9 17.0 %copy-start.17 = (f32[96,576]{0,1:T(8,128)S(1)}, f32[96,576]{0,1:T(8,128)}, u32[]{:S(2)}) copy-start(f32[96,576]{0,1:T(8,128)} %copy.45) | copy-start | bytes 663556
  324.3 12.2 %copy-start.19 = (f32[96,576]{0,1:T(8,128)S(1)}, f32[96,576]{0,1:T(8,128)}, u32[]{:S(2)}) copy-start(f32[96,576]{0,1:T(8,128)} %get-tuple-element.78) | copy-start | bytes 663556
  324.3 13.0 %copy-start.18 = (f32[96,576]{0,1:T(8,128)S(1)}, f32[96,576]{0,1:T(8,128)}, u32[]{:S(2)}) copy-start(f32[96,576]{0,1:T(8,128)} %get-tuple-element.79) | copy-start | bytes 663556
  338.2 4.4 %copy-start.7 = (bf16[1,768,768]{2,1,0:T(8,128)(2,1)S(1)}, bf16[1,768,768]{2,1,0:T(8,128)(2,1)}, u32[]{:S(2)}) copy-start(bf16[1,768,768]{2,1,0:T(8,128)(2,1)} %param.30) | copy-start | bytes 3538948
  342.6 12.4 %copy-start.15 = (bf16[192,768]{1,0:T(8,128)(2,1)S(1)}, bf16[192,768]{1,0:T(8,128)(2,1)}, u32[]{:S(2)}) copy-start(bf16[192,768]{1,0:T(8,128)(2,1)} %all_gather.13) | copy-start | bytes 884740
  344.4 13.7 %copy-start.14 = (bf16[768,768]{1,0:T(8,128)(2,1)S(1)}, bf16[768,768]{1,0:T(8,128)(2,1)}, u32[]{:S(2)}) copy-start(bf16[768,768]{1,0:T(8,128)(2,1)} %all-gather.5.cloned.1.call-done) | copy-start | bytes 3538948
  (12 other events, 21.7 us)
Sparse Core Ops, SparseCore 0:
  13.3 54.1 all-reduce.6
  101.0 126.5 all-reduce.8
  251.1 49.9 all-reduce.10
  303.1 25.3 all-gather.4
  330.9 24.0 all-gather.2
where the time goes:
time: 367 us; the launch traced here: 366 us
  waiting for transfers between devices  193 us (53%)
  blocking collectives  67 us (18%)
  matrix products  50.5 us (14%)
  other arithmetic  21.4 us (6%)
  between operations  17.4 us (5%)
  local copies, waits for them, and re-layouts  16.1 us (4%)
    psum x1, waiting for transfers between devices, pair_update(): left_col = lax.psum(part_col, ('dp', 'tensor')) / replicas  126 us
    dot_general x76, matrix products, matmul_high(): jnp.dot(left, right, precision=lax.Precision.HIGHEST, preferred_element_t...  50.5 us
    psum x1, waiting for transfers between devices, pair_update(): lax.psum(matmul_high(merged_col.T, normed_col).astype(jnp.bfloat16), 'dp')  35.7 us
    psum x1, blocking collectives, pair_update(): left_row = lax.psum(part_row, 'dp') / replicas  25.5 us
    psum x1, waiting for transfers between devices, pair_update(): left_row = lax.psum(part_row, 'dp') / replicas  20 us
    psum x1, blocking collectives, pair_update(): gram_row = lax.psum(matmul_high(left_row.T, left_row), 'tensor')  19 us
    unnamed x70, local copies, waits for them, and re-layouts  15.9 us
    all_gather x1, blocking collectives, pair_update(): lax.all_gather(master_row.astype(jnp.bfloat16), 'dp', axis=0, tiled=True)  11.7 us
  transfers between devices with their start and end apart: 5, of which 4 were waited for; matrix products, arithmetic and copies ran while one was open for 11% of the time, Pallas kernels for 0%

commit v1 on v0

--- a/solution.py
+++ b/solution.py
@@ -38,7 +38,7 @@
     merged_row = grad_row[0].astype(jnp.float32) + error_row[0]
     part_col = matmul_high(merged_col, basis_col)
     part_row = matmul_high(merged_row, basis_row)
-    left_col = lax.psum(part_col, ("dp", "tensor")) / replicas
+    left_col = lax.psum(lax.psum(part_col, "tensor"), "dp") / replicas
     left_row = lax.psum(part_row, "dp") / replicas
     gram_row = lax.psum(matmul_high(left_row.T, left_row), "tensor")
     gram_col = matmul_high(left_col.T, left_col)

time: 367 us -> 410 us (1.12)
  waiting for transfers between devices: 193 us -> 234 us
    psum x2 -> x3, waiting for transfers between devices: 146 us -> 173 us  [the longest x1 109 us: pair_update(): lax.psum(matmul_high(merged_row.T, normed_row), ('dp', 'tensor')) / replicas]
    all_gather x1, waiting for transfers between devices: 0.01 us -> 15.1 us  [pair_update(): lax.all_gather(master_row.astype(jnp.bfloat16), 'dp', axis=0, tiled=True)]
    all_gather x1, waiting for transfers between devices: 10.6 us -> 0.01 us  [pair_update(): lax.all_gather(master_col.astype(jnp.bfloat16), 'dp', axis=0, tiled=True)]
    psum x1, waiting for transfers between devices: 35.7 us -> 46.2 us  [pair_update(): lax.psum(matmul_high(merged_col.T, normed_col).astype(jnp.bfloat16), 'dp')]
    unnamed x70 -> x80, local copies, waits for them, and re-layouts: 15.9 us -> 18 us
  transfers between devices with their start and end apart: 5 -> 6, of which waited for: 4 -> 5; matrix products, arithmetic and copies ran while one was open for 11% -> 10% of each run, Pallas kernels for 0% -> 0%
where the time goes in v1:
time: 410 us; the launch traced here: 409 us
  waiting for transfers between devices  234 us (57%)
  blocking collectives  65.7 us (16%)
  matrix products  53.7 us (13%)
  local copies, waits for them, and re-layouts  19.7 us (5%)
  other arithmetic  17.8 us (4%)
  between operations  17.7 us (4%)
    psum x1, waiting for transfers between devices, pair_update(): lax.psum(matmul_high(merged_row.T, normed_row), ('dp', 'tensor')) / replicas  109 us
    psum x2, waiting for transfers between devices, pair_update(): left_col = lax.psum(lax.psum(part_col, 'tensor'), 'dp') / replicas  64.1 us
    dot_general x76, matrix products, matmul_high(): jnp.dot(left, right, precision=lax.Precision.HIGHEST, preferred_element_t...  53.7 us
    psum x1, waiting for transfers between devices, pair_update(): lax.psum(matmul_high(merged_col.T, normed_col).astype(jnp.bfloat16), 'dp')  46.2 us
    psum x1, blocking collectives, pair_update(): left_row = lax.psum(part_row, 'dp') / replicas  25.5 us
    psum x1, blocking collectives, pair_update(): gram_row = lax.psum(matmul_high(left_row.T, left_row), 'tensor')  19 us
    unnamed x80, local copies, waits for them, and re-layouts  18 us
    all_gather x1, waiting for transfers between devices, pair_update(): lax.all_gather(master_row.astype(jnp.bfloat16), 'dp', axis=0, tiled=True)  15.1 us
  transfers between devices with their start and end apart: 6, of which 5 were waited for; matrix products, arithmetic and copies ran while one was open for 10% of the time, Pallas kernels for 0%

profile of v1, /device:TPU:0, one launch (start us, length us, event | category | flops | bytes accessed | tf_op | source)
XLA Modules:
  0.0 409.3 jit_solution(13117735565475752050)
XLA Ops:
  7.3 3.7 fusion.12
  11.0 4.3 %fusion.7 = f32[768,32]{0,1:T(8,128)} fusion(f32[768,32]{0,1:T(8,128)S(1)} %copy-done, f32[1,768,768]{2,1,0:T(8,128)S(1)} %copy-done.1, bf16[1,768,768]{2,1,0:T(8,128)(2,1)} %param.30), kind=kOutput, calls=%fused_computation.9 | convolution fusion | flops 227672064 | bytes 3735552 | tf_op jit(solution)/shard_map/dot_general | solution.py:12
  16.1 25.5 %psum.87 = f32[192,32]{0,1:T(8,128)S(1)} all-reduce(f32[192,32]{0,1:T(8,128)S(1)} %fusion.43), channel_id=1, replica_groups=mesh['dp'=8,'tensor'=4] {'dp'}, use_global_device_ids=true, to_apply=%region_4.0 | all-reduce | flops 6144 | bytes 49152 | tf_op jit(solution)/shard_map/psum | solution.py:42
  41.6 5.0 %fusion.2 = f32[768,32]{0,1:T(8,128)} fusion(f32[768,32]{0,1:T(8,128)} %param.37, f32[1,768,768]{2,1,0:T(8,128)} %param.36, bf16[1,768,768]{2,1,0:T(8,128)(2,1)} %param.35), kind=kOutput, calls=%fused_computation.3 | convolution fusion | flops 227672064 | bytes 3735552 | tf_op jit(solution)/shard_map/dot_general | solution.py:12
  46.6 6.5 %all-reduce.14.cloned.1.call-done = (f32[768,32]{0,1:T(8,128)}, f32[768,32]{0,1:T(8,128)}) async-done(((f32[768,32]{0,1:T(8,128)}, f32[768,32]{0,1:T(8,128)}), (f32[768,32]{0,1:T(8,128)}, f32[768,32]{0,1:T(8,128)})) %all-reduce.14.cloned.1.call-update) | async-done | bytes 196624 | tf_op jit(solution)/shard_map/psum | solution.py:41
  53.4 57.6 %all-reduce.12.cloned.1.call-done = (f32[768,32]{0,1:T(8,128)}, f32[768,32]{0,1:T(8,128)}, f32[768,32]{0,1:T(8,128)}) async-done(((f32[768,32]{0,1:T(8,128)}, f32[768,32]{0,1:T(8,128)}, f32[768,32]{0,1:T(8,128)}), (f32[768,32]{0,1:T(8,128)}, f32[768,32]{0,1:T(8,128)}, f32[768,32]{0,1:T(8,128)})) %all-reduce.12.cloned.1.call-update) | async-done | bytes 294928 | tf_op jit(solution)/shard_map/psum | solution.py:41
  112.3 19.0 %all-reduce.2 = (f32[32,32]{1,0:T(8,128)S(1)}, f32[32,32]{1,0:T(8,128)S(1)}) all-reduce(f32[32,32]{1,0:T(8,128)S(1)} %fusion.66, f32[32,32]{1,0:T(8,128)S(1)} %fusion.48), channel_id=1, replica_groups=mesh['dp'=8,'tensor'=4] {'tensor'}, use_global_device_ids=true, to_apply=%region_5.0 | all-reduce | flops 2048 | bytes 16384 | tf_op jit(solution)/shard_map/psum | solution.py:43
  149.3 4.2 %fusion = f32[768,32]{0,1:T(8,128)} fusion(f32[768,32]{0,1:T(8,128)S(1)} %fusion.46, f32[1,768,768]{2,1,0:T(8,128)} %param.36, bf16[1,768,768]{2,1,0:T(8,128)(2,1)} %param.35), kind=kOutput, calls=%fused_computation.1 | convolution fusion | flops 227672064 | bytes 3735552 | tf_op jit(solution)/shard_map/dot_general | solution.py:12
  159.1 2.3 fusion.15
  162.0 2.3 fusion.18
  164.4 2.3 fusion.41
  166.7 46.2 %all-reduce.16.cloned.1.call-done = (bf16[576,32]{0,1:T(8,128)(2,1)}, bf16[768,32]{0,1:T(8,128)(2,1)}) async-done(((bf16[576,32]{0,1:T(8,128)(2,1)}, bf16[768,32]{0,1:T(8,128)(2,1)}), (bf16[576,32]{0,1:T(8,128)(2,1)}, bf16[768,32]{0,1:T(8,128)(2,1)})) %all-reduce.16.cloned.1.call-update) | async-done | bytes 86032 | tf_op jit(solution)/shard_map/psum | solution.py:48
  214.5 2.9 fusion.110
  220.1 1.8 copy.44
  227.9 2.1 fusion.89
  231.7 3.5 fusion.14
  235.2 108.6 %all-reduce.10.cloned.1.call-done = (f32[768,32]{0,1:T(8,128)}, f32[768,32]{0,1:T(8,128)}) async-done(((f32[768,32]{0,1:T(8,128)}, f32[768,32]{0,1:T(8,128)}), (f32[768,32]{0,1:T(8,128)}, f32[768,32]{0,1:T(8,128)})) %all-reduce.10.cloned.1.call-update) | async-done | bytes 196624 | tf_op jit(solution)/shard_map/psum | solution.py:53
  344.7 2.0 fusion.117
  349.1 11.8 %all_gather.12 = bf16[768,576]{1,0:T(8,128)(2,1)S(1)} all-gather(bf16[96,576]{1,0:T(8,128)(2,1)} %copy.46), channel_id=1, replica_groups=mesh['dp'=8,'tensor'=4] {'dp'}, dimensions={0}, use_global_device_ids=true | all-gather | bytes 995328 | tf_op jit(solution)/shard_map/all_gather | solution.py:63
  362.2 1.8 copy.47
  365.9 3.9 fusion.9
  371.2 9.4 %all_gather.13 = bf16[192,768]{1,0:T(8,128)(2,1)S(1)} all-gather(bf16[24,768]{1,0:T(8,128)(2,1)S(1)} %get-tuple-element.77), channel_id=1, replica_groups=mesh['dp'=8,'tensor'=4] {'dp'}, dimensions={0}, use_global_device_ids=true | all-gather | bytes 331776 | tf_op jit(solution)/shard_map/all_gather | solution.py:64
  383.3 15.1 %all-gather.5.cloned.1.call-done = bf16[768,768]{1,0:T(8,128)(2,1)} async-done(((bf16[96,768]{1,0:T(8,128)(2,1)}), bf16[768,768]{1,0:T(8,128)(2,1)}) %all-gather.5.cloned.1.call-update) | async-done | bytes 1179664 | tf_op jit(solution)/shard_map/all_gather | solution.py:64
  399.1 2.4 copy.63
  (168 shorter events, 47.2 us)
Async XLA Ops:
  7.2 45.9 %all-reduce.14.cloned.1.call-start = ((), (), s32[]{:S(2)}) async-start(), calls=%async_computation.4 | async-start | bytes 393216 | tf_op jit(solution)/shard_map/psum | solution.py:41
  15.4 95.6 %all-reduce.12.cloned.1.call-start = ((), (), s32[]{:S(2)}) async-start(), calls=%async_computation.3 | async-start | bytes 589824 | tf_op jit(solution)/shard_map/psum | solution.py:41
  41.6 11.8 %copy-start.25 = (f32[192,32]{0,1:T(8,128)}, f32[192,32]{0,1:T(8,128)S(1)}, u32[]{:S(2)}) copy-start(f32[192,32]{0,1:T(8,128)S(1)} %psum.87) | copy-start | bytes 73732
  53.2 159.8 %all-reduce.16.cloned.1.call-start = ((), (), s32[]{:S(2)}) async-start(), calls=%async_computation.5 | async-start | bytes 180224 | tf_op jit(solution)/shard_map/psum | solution.py:48
  111.0 38.0 %copy-start.21 = (f32[768,32]{0,1:T(8,128)S(1)}, f32[768,32]{0,1:T(8,128)}, u32[]{:S(2)}) copy-start(f32[768,32]{0,1:T(8,128)} %get-tuple-element.63) | copy-start | bytes 294916
  146.2 12.6 %copy-start.20 = (f32[768,32]{0,1:T(8,128)S(1)}, f32[768,32]{0,1:T(8,128)}, u32[]{:S(2)}) copy-start(f32[768,32]{0,1:T(8,128)} %get-tuple-element.64) | copy-start | bytes 294916
  148.7 10.4 %copy-start.7 = (bf16[1,768,768]{2,1,0:T(8,128)(2,1)S(1)}, bf16[1,768,768]{2,1,0:T(8,128)(2,1)}, u32[]{:S(2)}) copy-start(bf16[1,768,768]{2,1,0:T(8,128)(2,1)} %param.30) | copy-start | bytes 3538948
  153.5 7.8 %copy-start.34 = (f32[32,32]{1,0:T(8,128)S(1)}, f32[32,32]{1,0:T(8,128)}, u32[]{:S(2)}) copy-start(f32[32,32]{1,0:T(8,128)} %fusion.95) | copy-start | bytes 12292
  153.6 7.8 %copy-start.35 = (f32[32,32]{1,0:T(8,128)S(1)}, f32[32,32]{1,0:T(8,128)}, u32[]{:S(2)}) copy-start(f32[32,32]{1,0:T(8,128)} %fusion.94) | copy-start | bytes 12292
  153.6 8.1 %copy-start.19 = (f32[768,32]{0,1:T(8,128)S(1)}, f32[768,32]{0,1:T(8,128)}, u32[]{:S(2)}) copy-start(f32[768,32]{0,1:T(8,128)} %get-tuple-element.62) | copy-start | bytes 294916
  153.6 8.4 %copy-start.3 = (f32[1,768,576]{1,2,0:T(8,128)S(1)}, f32[1,768,576]{1,2,0:T(8,128)}, u32[]{:S(2)}) copy-start(f32[1,768,576]{1,2,0:T(8,128)} %param.21) | copy-start | bytes 5308420
  153.6 8.4 %copy-start.10 = (bf16[1,768,576]{1,2,0:T(8,128)(2,1)S(1)}, bf16[1,768,576]{1,2,0:T(8,128)(2,1)}, u32[]{:S(2)}) copy-start(bf16[1,768,576]{1,2,0:T(8,128)(2,1)} %param.20) | copy-start | bytes 2654212
  164.3 179.5 %all-reduce.10.cloned.1.call-start = ((), (), s32[]{:S(2)}) async-start(), calls=%async_computation.2 | async-start | bytes 393216 | tf_op jit(solution)/shard_map/psum | solution.py:53
  166.7 216.6 %all-gather.3.cloned.1.call-start = ((), (), s32[]{:S(2)}) async-start(), calls=%async_computation | async-start | bytes 1327104 | tf_op jit(solution)/shard_map/all_gather | solution.py:63
  219.8 178.6 %all-gather.5.cloned.1.call-start = ((), (), s32[]{:S(2)}) async-start(), calls=%async_computation.1 | async-start | bytes 1327104 | tf_op jit(solution)/shard_map/all_gather | solution.py:64
  235.2 113.0 %copy-start.28 = (f32[96,768]{1,0:T(8,128)S(1)}, f32[96,768]{1,0:T(8,128)}, u32[]{:S(2)}) copy-start(f32[96,768]{1,0:T(8,128)} %param.38) | copy-start | bytes 884740
  235.2 113.0 %copy-start.29 = (f32[96,768]{1,0:T(8,128)S(1)}, f32[96,768]{1,0:T(8,128)}, u32[]{:S(2)}) copy-start(f32[96,768]{1,0:T(8,128)} %param.39) | copy-start | bytes 884740
  344.7 16.3 %copy-start.18 = (f32[768,32]{0,1:T(8,128)}, f32[768,32]{0,1:T(8,128)S(1)}, u32[]{:S(2)}) copy-start(f32[768,32]{0,1:T(8,128)S(1)} %broadcast_multiply_fusion) | copy-start | bytes 294916
  365.8 14.8 %copy-start.12 = (f32[1,192,768]{2,1,0:T(8,128)S(1)}, f32[1,192,768]{2,1,0:T(8,128)}, u32[]{:S(2)}) copy-start(f32[1,192,768]{2,1,0:T(8,128)} %param.26) | copy-start | bytes 1769476
  365.9 14.7 %copy-start.14 = (bf16[1,192,768]{2,1,0:T(8,128)(2,1)S(1)}, bf16[1,192,768]{2,1,0:T(8,128)(2,1)}, u32[]{:S(2)}) copy-start(bf16[1,192,768]{2,1,0:T(8,128)(2,1)} %param.25) | copy-start | bytes 884740
  365.9 15.6 %copy-start.6 = (f32[768,768]{1,0:T(8,128)S(1)}, f32[768,768]{1,0:T(8,128)}, u32[]{:S(2)}) copy-start(f32[768,768]{1,0:T(8,128)} %copy-done.5) | copy-start | bytes 7077892
  369.8 11.7 %copy-start.2 = (f32[1,768,768]{2,1,0:T(8,128)S(1)}, f32[1,768,768]{2,1,0:T(8,128)}, u32[]{:S(2)}) copy-start(f32[1,768,768]{2,1,0:T(8,128)} %param.36) | copy-start | bytes 7077892
  369.8 11.7 %copy-start.8 = (bf16[1,768,768]{2,1,0:T(8,128)(2,1)S(1)}, bf16[1,768,768]{2,1,0:T(8,128)(2,1)}, u32[]{:S(2)}) copy-start(bf16[1,768,768]{2,1,0:T(8,128)(2,1)} %param.35) | copy-start | bytes 3538948
  369.8 13.5 %copy-start.22 = (f32[768,32]{0,1:T(8,128)}, f32[768,32]{0,1:T(8,128)S(1)}, u32[]{:S(2)}) copy-start(f32[768,32]{0,1:T(8,128)S(1)} %broadcast_multiply_fusion.1) | copy-start | bytes 294916
  (18 other events, 60.8 us)
Sparse Core Ops, SparseCore 0:
  15.5 37.6 all-reduce.13
  57.6 53.3 all-reduce.11
  164.5 48.4 all-reduce.15
  219.6 124.1 all-reduce.9
  346.1 25.8 all-gather.2
  374.3 24.0 all-gather.4
